TPU v7x, 32 devices: a whole 2x2x4 slice. The times are simulated.
32 devices in a mesh: section: 4 (over x, core), sp: 8 (over z, y).
Axes of the slice: x: 2, y: 2, z: 4, core: 2. Of those that a mesh axis runs over, the one named last changes fastest.
Arguments:
- field_in: bfloat16 [4, 384, 192, 768], P('section', 'sp'), may hold values from -6 to 6
- spectral_gain: bfloat16 [4, 192], P('section'), may hold values from 0.5 to 1.5
- spectral_weight: bfloat16 [4, 384, 192, 384], P('section', 'sp'), may hold values from -0.3125 to 0.3125
- mixer_gain: bfloat16 [4, 192], P('section'), may hold values from 0.5 to 1.5
- up_weight: bfloat16 [4, 192, 384], P('section'), may hold values from -0.4375 to 0.4375
- up_bias: bfloat16 [4, 384], P('section'), may hold values from -3 to 3
- down_weight: bfloat16 [4, 192, 384], P('section'), may hold values from -0.3125 to 0.3125
Outputs:
- next_field: bfloat16 [4, 384, 192, 768], P('section', 'sp')
All inputs are finite; a program needn't handle non-finite values.
Results may differ from a plain program's by a relative error of at most 0.012.
Values may be sent and summed in bfloat16 or wider, within the bound.
A program may use at most 192 MiB of HBM per device.

v0:
```python
import math
import jax
import jax.numpy as jnp
from jax import lax
from jax.sharding import PartitionSpec as P

C = 192
NLAT = 384
NLON = 768
LMAX = 384
MMAX = 384
CHUNKS = 4
EPSILON = 1e-05


def passed_along(value, axis, by):
    count = lax.axis_size(axis)
    return lax.ppermute(value, axis, [(i, (i + by) % count) for i in range(count)])


def quad_weights(cycle_index, cycle_count):
    terms_count = cycle_count // 2
    orders = jnp.arange(1, terms_count + 1, dtype=jnp.int32)
    phase_turns = orders[None, :] * (2 * cycle_index[:, None] + 1) % (2 * cycle_count)
    angles = math.pi * phase_turns.astype(jnp.float32) / cycle_count
    orders_real = orders.astype(jnp.float32)
    series = jnp.sum(jnp.cos(angles) / (4.0 * orders_real * orders_real - 1.0)[None, :], axis=1)
    return 2.0 / cycle_count * (1.0 - 2.0 * series)


def fourier_tables(point_count, orders):
    points = jnp.arange(point_count, dtype=jnp.int32)
    phase_turns = points[:, None] * orders[None, :] % point_count
    angles = 2.0 * math.pi / point_count * phase_turns.astype(jnp.float32)
    cosines = jnp.cos(angles)
    sine_values = jnp.sin(angles)
    forward = jnp.stack([cosines, -sine_values], axis=1).astype(jnp.bfloat16)
    doubling = jnp.where(orders == 0, 1.0, 2.0).astype(jnp.float32)[:, None]
    inverse = jnp.stack([cosines.T * doubling, -sine_values.T * doubling], axis=0).astype(
        jnp.bfloat16
    )
    return (forward, inverse)


def step_entries(degree, order_col, cosines):
    active = degree >= order_col + 1.0
    further = degree >= order_col + 2.0
    degree_sq = degree * degree
    order_sq = order_col * order_col
    lead_coeff = jnp.sqrt(
        jnp.where(
            active, (4.0 * degree_sq - 1.0) / jnp.where(active, degree_sq - order_sq, 1.0), 0.0
        )
    )
    before = degree - 1.0
    before_sq = before * before
    trail_coeff = jnp.sqrt(
        jnp.where(
            further, (before_sq - order_sq) / jnp.where(further, 4.0 * before_sq - 1.0, 1.0), 0.0
        )
    )
    diag_top = jnp.where(active, lead_coeff * cosines, 1.0)
    off_top = jnp.where(active, -lead_coeff * trail_coeff, 0.0)
    off_low = jnp.where(active, 1.0, 0.0)
    diag_low = jnp.where(active, 0.0, 1.0)
    return (diag_top, off_top, off_low, diag_low)


def legendre_rows(order_index, cycle_count, degree_count):
    colatitude = math.pi * (jnp.arange(cycle_count, dtype=jnp.float32) + 0.5) / cycle_count
    cosines = jnp.cos(colatitude)[None, None, :]
    sine_values = jnp.sin(colatitude)
    order_real = order_index.astype(jnp.float32)
    steps_all = jnp.arange(1, degree_count + 1, dtype=jnp.float32)
    factors = jnp.log((2.0 * steps_all - 1.0) / (2.0 * steps_all))
    below_mask = (steps_all[None, :] <= order_real[:, None]).astype(jnp.float32)
    partial_log = jnp.sum(below_mask * factors[None, :], axis=1)
    start_log = 0.5 * jnp.log((2.0 * order_real + 1.0) / (4.0 * math.pi)) + 0.5 * partial_log
    start_log = start_log[:, None] + order_real[:, None] * jnp.log(sine_values)[None, :]
    order_col = order_real[None, :, None]
    block_count = degree_count // 16
    block_base = (16 * jnp.arange(block_count, dtype=jnp.int32)).astype(jnp.float32)[:, None, None]
    shape_all = (block_count, order_index.shape[0], cycle_count)
    unit_array = jnp.ones(shape_all, jnp.float32)
    zero_array = jnp.zeros(shape_all, jnp.float32)

    def product_half(half_turn, matrices):
        upper_left, upper_right, lower_left, lower_right, log_scale = matrices
        for inner_step in range(8):
            degree = block_base + (half_turn * 8 + inner_step).astype(jnp.float32)
            diag_top, off_top, off_low, diag_low = step_entries(degree, order_col, cosines)
            next_ul = diag_top * upper_left + off_top * lower_left
            next_ur = diag_top * upper_right + off_top * lower_right
            next_ll = off_low * upper_left + diag_low * lower_left
            next_lr = off_low * upper_right + diag_low * lower_right
            largest = jnp.maximum(
                jnp.maximum(jnp.abs(next_ul), jnp.abs(next_ur)),
                jnp.maximum(jnp.abs(next_ll), jnp.abs(next_lr)),
            )
            upper_left = next_ul / largest
            upper_right = next_ur / largest
            lower_left = next_ll / largest
            lower_right = next_lr / largest
            log_scale = log_scale + jnp.log(largest)
        return (upper_left, upper_right, lower_left, lower_right, log_scale)

    products = lax.fori_loop(
        0, 2, product_half, (unit_array, zero_array, zero_array, unit_array, zero_array)
    )

    def carry_block(vector_state, block_matrix):
        lead_value, lag_value, log_value = vector_state
        upper_left, upper_right, lower_left, lower_right, log_scale = block_matrix
        next_lead = upper_left * lead_value + upper_right * lag_value
        next_lag = lower_left * lead_value + lower_right * lag_value
        largest = jnp.maximum(jnp.abs(next_lead), jnp.abs(next_lag))
        return (
            (next_lead / largest, next_lag / largest, log_value + log_scale + jnp.log(largest)),
            vector_state,
        )

    initial = (unit_array[0], zero_array[0], start_log)
    final_state, starts = lax.scan(carry_block, initial, products)

    def degree_half(vector_state, half_turn):
        lead_value, lag_value, log_value = vector_state
        values = []
        for inner_step in range(8):
            degree = block_base + (half_turn * 8 + inner_step).astype(jnp.float32)
            diag_top, off_top, off_low, diag_low = step_entries(degree, order_col, cosines)
            next_lead = diag_top * lead_value + off_top * lag_value
            next_lag = off_low * lead_value + diag_low * lag_value
            largest = jnp.maximum(jnp.abs(next_lead), jnp.abs(next_lag))
            lead_value = next_lead / largest
            lag_value = next_lag / largest
            log_value = log_value + jnp.log(largest)
            values.append(lead_value * jnp.exp(log_value))
        return ((lead_value, lag_value, log_value), jnp.stack(values))

    last_state, table_rows = lax.scan(degree_half, starts, jnp.arange(2, dtype=jnp.int32))
    legendre = jnp.transpose(table_rows, (3, 2, 0, 1, 4)).reshape(
        order_index.shape[0], degree_count, cycle_count
    )
    degrees = jnp.arange(degree_count, dtype=jnp.int32)
    return jnp.where(degrees[None, :, None] >= order_index[:, None, None], legendre, 0.0)


def layer_norm(values, gain_row):
    values = values.astype(jnp.float32)
    average = jnp.mean(values, axis=-2, keepdims=True)
    centred = values - average
    variance = jnp.mean(centred * centred, axis=-2, keepdims=True)
    return centred * lax.rsqrt(variance + EPSILON) * gain_row.astype(jnp.float32)[:, None]


def mixing_matrix(weight):
    width = weight.shape[1]
    real_weight = weight[:, :, :width]
    imag_weight = weight[:, :, width:]
    top_half = jnp.concatenate([real_weight, imag_weight], axis=2)
    bottom_half = jnp.concatenate([-imag_weight, real_weight], axis=2)
    return jnp.concatenate([top_half, bottom_half], axis=1)


def order_list(sp_count, modes_dev):
    slots = jnp.arange(MMAX, dtype=jnp.int32)
    owner = slots // modes_dev
    within = slots % modes_dev
    mirrored = jnp.where(within % 2 == 0, owner, sp_count - 1 - owner)
    return within * sp_count + mirrored


def triangle_plan(sp_count, half):
    plan = []
    for rank in range(sp_count):
        low_block = min(rank, sp_count - 1 - rank)
        high_block = sp_count - 1 - low_block
        low_half = 0 if rank == low_block else 1
        low_start = (2 * low_block + low_half) * half
        high_start = (2 * high_block + 1 - low_half) * half
        low_count = (low_start + half - 1) // sp_count + 1
        high_count = (high_start + half - 1) // sp_count + 1
        plan.append((low_start, low_count, high_start, high_count))
    slots = max((entry[1] + entry[3] for entry in plan))
    return (plan, slots)


def shards(field_in, spectral_gain, spectral_weight, mixer_gain, up_weight, up_bias, down_weight):
    grid_values = field_in[0]
    cycle_rows = grid_values.shape[0]
    sp_count = lax.axis_size("sp")
    device_rank = lax.axis_index("sp")
    modes_dev = MMAX // sp_count
    all_orders = order_list(sp_count, modes_dev)
    order_index = lax.dynamic_slice_in_dim(all_orders, device_rank * modes_dev, modes_dev, 0)
    cycle_index = device_rank * cycle_rows + jnp.arange(cycle_rows, dtype=jnp.int32)
    legendre = legendre_rows(order_index, NLAT, LMAX).astype(jnp.bfloat16)
    forward, inverse = fourier_tables(NLON, all_orders)
    weighting = quad_weights(cycle_index, NLAT) * (2.0 * math.pi / NLON)
    normed = layer_norm(grid_values, spectral_gain[0]).astype(jnp.bfloat16)
    spectral = jnp.einsum("nrm,acn->marc", forward, normed, preferred_element_type=jnp.float32)
    spectral = (
        (spectral * weighting[None, :, None, None])
        .astype(jnp.bfloat16)
        .reshape(MMAX, cycle_rows, 2 * C)
    )
    coeffs = jnp.einsum(
        "mla,mak->mlk",
        legendre,
        lax.all_to_all(spectral, "sp", split_axis=0, concat_axis=1, tiled=True),
        preferred_element_type=jnp.float32,
    ).astype(jnp.bfloat16)
    half = LMAX // sp_count // 2
    plan, slots = triangle_plan(sp_count, half)
    own_weight = spectral_weight[0]
    partner = [(i, sp_count - 1 - i) for i in range(sp_count)]
    other_weight = lax.ppermute(own_weight[half:], "sp", partner)
    is_low = device_rank < sp_count // 2
    low_weight = mixing_matrix(jnp.where(is_low, own_weight[:half], other_weight))
    high_weight = mixing_matrix(jnp.where(is_low, other_weight, own_weight[:half]))
    width = coeffs.shape[2]
    pieces = []
    for low_start, low_count, high_start, high_count in plan:
        pieces.append(coeffs[:low_count, low_start : low_start + half])
        gap = slots - low_count - high_count
        if gap:
            pieces.append(jnp.zeros((gap, half, width), coeffs.dtype))
        pieces.append(coeffs[:high_count, high_start : high_start + half])
    packed = jnp.concatenate(pieces, axis=0)
    by_degree = lax.all_to_all(packed, "sp", split_axis=0, concat_axis=0, tiled=True)
    by_degree = by_degree.reshape(sp_count, slots, half, width)
    most_low = max((entry[1] for entry in plan))
    most_high = max((entry[3] for entry in plan))
    low_mixed = jnp.einsum(
        "dslk,lkj->dslj", by_degree[:, :most_low], low_weight, preferred_element_type=jnp.float32
    ).astype(jnp.bfloat16)
    high_mixed = jnp.einsum(
        "dslk,lkj->dslj",
        by_degree[:, slots - most_high :],
        high_weight,
        preferred_element_type=jnp.float32,
    ).astype(jnp.bfloat16)
    low_rows = jnp.array([entry[1] for entry in plan], jnp.int32)[device_rank]
    row = jnp.arange(slots, dtype=jnp.int32)[None, :, None, None]
    mixed = jnp.where(
        row < low_rows,
        jnp.pad(low_mixed, ((0, 0), (0, slots - most_low), (0, 0), (0, 0))),
        jnp.pad(high_mixed, ((0, 0), (slots - most_high, 0), (0, 0), (0, 0))),
    )
    returned = lax.all_to_all(
        mixed.reshape(sp_count * slots, half, width), "sp", split_axis=0, concat_axis=0, tiled=True
    ).reshape(sp_count, slots, half, width)
    parts = {}
    for rank, (low_start, low_count, high_start, high_count) in enumerate(plan):
        parts[low_start] = (returned[rank, :low_count], low_count)
        parts[high_start] = (returned[rank, slots - high_count :], high_count)
    mixed_coeffs = jnp.concatenate(
        [
            jnp.pad(parts[start][0], ((0, modes_dev - parts[start][1]), (0, 0), (0, 0)))
            for start in sorted(parts)
        ],
        axis=1,
    )
    grid_part = jnp.einsum(
        "mla,mlk->mak", legendre, mixed_coeffs, preferred_element_type=jnp.float32
    ).astype(jnp.bfloat16)
    grid_part = grid_part.reshape(modes_dev, sp_count, cycle_rows, width)
    chunk = cycle_rows // CHUNKS
    outputs = []
    for start in range(0, cycle_rows, chunk):
        on_grid = lax.all_to_all(
            grid_part[:, :, start : start + chunk].reshape(modes_dev, sp_count * chunk, width),
            "sp",
            split_axis=1,
            concat_axis=0,
            tiled=True,
        )
        synthesis = jnp.einsum(
            "marc,rmn->acn",
            on_grid.reshape(MMAX, chunk, 2, C),
            inverse,
            preferred_element_type=jnp.float32,
        )
        residual = grid_values[start : start + chunk].astype(jnp.float32) + synthesis
        hidden_in = layer_norm(residual, mixer_gain[0]).astype(jnp.bfloat16)
        hidden = jnp.einsum(
            "acn,ch->anh", hidden_in, up_weight[0], preferred_element_type=jnp.float32
        ) + up_bias[0].astype(jnp.float32)
        hidden = jax.nn.gelu(hidden, approximate=False).astype(jnp.bfloat16)
        branch = jnp.einsum(
            "anh,ch->acn", hidden, down_weight[0], preferred_element_type=jnp.float32
        )
        result = (residual + branch).astype(jnp.bfloat16)
        outputs.append(passed_along(result, "section", 1))
    return jnp.concatenate(outputs, axis=0)[None]


def solution(mesh):
    in_specs = (
        P("section", "sp", None, None),
        P("section", None),
        P("section", "sp", None, None),
        P("section", None),
        P("section", None, None),
        P("section", None),
        P("section", None, None),
    )
    out_specs = P("section", "sp", None, None)
    return jax.shard_map(shards, mesh=mesh, in_specs=in_specs, out_specs=out_specs, check_vma=False)
```

profile of v0, /device:TPU:0, one launch (start us, length us, event | category | flops | bytes accessed | tf_op | source)
XLA Modules:
  0.0 1701.2 jit_solution(16613426593756830060)
XLA Ops:
  24.8 19.0 %multiply_convert_fusion = bf16[48,192,2,384]{3,1,2,0:T(8,128)(2,1)} fusion(f32[48]{0:T(128)S(1)} %subtract_multiply_fusion, bf16[1,48,192,768]{3,2,1,0:T(8,128)(2,1)} %param.14, f32[192]{0:T(256)S(1)} %bitcast.620, f32[48,768]{1,0:T(8,128)S(1)} %add_rsqrt_fusion, f32[48,768]{1,0:T(8,128)S(1)} %broadcast_multiply_fusion, ...), kind=kOutput, calls=%fused_computation.485 | convolution fusion | flops 10923540480 | bytes 29787072 | tf_op jit(solution)/shard_map/nrm,acn->marc/dot_general | solution.py:201
  43.8 18.6 %copy.34 = bf16[384,48,384]{2,1,0:T(8,128)(2,1)} copy(bf16[384,48,384]{0,2,1:T(8,128)(2,1)} %bitcast.601) | data formatting | bytes 28311552 | tf_op jit(solution)/shard_map/reshape | solution.py:205
  72.0 59.7 %while.70 = (s32[]{:T(128)}, f32[24,48,384]{2,1,0:T(8,128)}, f32[24,48,384]{2,1,0:T(8,128)}, f32[24,48,384]{2,1,0:T(8,128)}, f32[24,48,384]{2,1,0:T(8,128)}, /*i...) while((s32[]{:T(128)}, f32[24,48,384]{2,1,0:T(8,128)}, ...), condition=%wide.region_2.3_spmd.clone.clone, body=%wide.region_1.2_spmd.clone.clone.sunk | while | flops 123129520 | bytes 200388496 | solution.py:107
  132.4 58.0 %while.69 = (s32[]{:T(128)}, f32[48,384]{1,0:T(8,128)S(1)}, f32[48,384]{1,0:T(8,128)S(1)}, f32[48,384]{1,0:T(8,128)S(1)}, f32[24,48,384]{2,1,0:T(8,128)}, /*inde...) while((s32[]{:T(128)}, f32[48,384]{1,0:T(8,128)S(1)}, ...), condition=%wide.region_4.5_spmd.clone, body=%wide.region_3.4_spmd.clone.sunk | while | flops 368643 | bytes 1548453 | solution.py:123
  190.5 100.2 %while.68 = (s32[]{:T(128)}, f32[24,48,384]{2,1,0:T(8,128)}, f32[24,48,384]{2,1,0:T(8,128)}, f32[24,48,384]{2,1,0:T(8,128)S(1)}, bf16[2,8,24,48,384]{4,1,0,2,3:T...) while((s32[]{:T(128)}, f32[24,48,384]{2,1,0:T(8,128)}, ...), condition=%wide.region_6.7_spmd.clone.clone, body=%wide.region_5.6_spmd.clone.clone.sunk | while | flops 100568752 | bytes 101660528 | solution.py:140
  290.7 14.3 fusion.186
  305.0 71.5 %all-to-all-done = bf16[384,48,384]{2,1,0:T(8,128)(2,1)} async-done(((bf16[384,48,384]{2,1,0:T(8,128)(2,1)}), bf16[384,48,384]{2,1,0:T(8,128)(2,1)}, u32[]{:S(2)}, u32[]{:S(2)}) %all-to-all-start) | async-done | bytes 14155808 | tf_op jit(solution)/shard_map/all_to_all | solution.py:210
  389.4 19.7 %convolution_convert_fusion.1 = bf16[48,384,384]{2,1,0:T(8,128)(2,1)} fusion(bf16[48,384,384]{2,1,0:T(8,128)(2,1)} %fusion.186, bf16[48,384,384]{2,1,0:T(8,128)(2,1)} %bitcast.579), kind=kOutput, calls=%fused_computation.578 | convolution fusion | flops 5442895872 | bytes 42467328 | tf_op jit(solution)/shard_map/mla,mak->mlk/dot_general | solution.py:207
  453.3 191.3 %collective-permute-done = bf16[24,192,384]{2,1,0:T(8,128)(2,1)} collective-permute-done((bf16[24,192,384]{2,1,0:T(8,128)(2,1)}, bf16[24,192,384]{2,1,0:T(8,128)(2,1)}, u32[]{:S(2)}, u32[]{:S(2)}) %collective-permute-start) | collective-permute-done | bytes 3538976 | tf_op jit(solution)/shard_map/ppermute | solution.py:217
  655.4 29.7 %all-to-all-done.1 = bf16[408,24,384]{2,1,0:T(8,128)(2,1)} async-done(((bf16[408,24,384]{2,1,0:T(8,128)(2,1)}), bf16[408,24,384]{2,1,0:T(8,128)(2,1)}, u32[]{:S(2)}, u32[]{:S(2)}) %all-to-all-start.1) | async-done | bytes 7520288 | tf_op jit(solution)/shard_map/all_to_all | solution.py:230
  697.1 15.2 fusion.237
  751.7 252.8 %all_to_all.88 = bf16[408,24,384]{2,1,0:T(8,128)(2,1)S(1)} all-to-all(bf16[408,24,384]{2,1,0:T(8,128)(2,1)S(1)} %bitcast.596), channel_id=1, replica_groups=mesh['section'=4,'sp'=8] {'sp'}, dimensions={0} | all-to-all | bytes 15040512 | tf_op jit(solution)/shard_map/all_to_all | solution.py:250
  1021.1 19.2 %convolution_convert_fusion = bf16[48,384,384]{2,1,0:T(8,128)(2,1)} fusion(bf16[48,384,384]{2,1,0:T(8,128)(2,1)} %fusion.186, bf16[48,384,384]{2,1,0:T(8,128)(2,1)} %fusion.307), kind=kOutput, calls=%fused_computation.577 | convolution fusion | flops 5442895872 | bytes 42467328 | tf_op jit(solution)/shard_map/mla,mlk->mak/dot_general | solution.py:264
  1040.3 14.2 fusion.482
  1069.2 72.0 %all-to-all-done.5 = bf16[48,96,384]{2,0,1:T(8,128)(2,1)} async-done(((bf16[48,96,384]{2,0,1:T(8,128)(2,1)}), bf16[48,96,384]{2,0,1:T(8,128)(2,1)}, u32[]{:S(2)}, u32[]{:S(2)}) %all-to-all-start.5) | async-done | bytes 3538976 | tf_op jit(solution)/shard_map/all_to_all | solution.py:271
  1152.4 71.9 %all-to-all-done.3 = bf16[48,96,384]{2,0,1:T(8,128)(2,1)} async-done(((bf16[48,96,384]{2,0,1:T(8,128)(2,1)}), bf16[48,96,384]{2,0,1:T(8,128)(2,1)}, u32[]{:S(2)}, u32[]{:S(2)}) %all-to-all-start.3) | async-done | bytes 3538976 | tf_op jit(solution)/shard_map/all_to_all | solution.py:271
  1235.0 72.4 %all-to-all-done.6 = bf16[48,96,384]{2,0,1:T(8,128)(2,1)} async-done(((bf16[48,96,384]{2,0,1:T(8,128)(2,1)}), bf16[48,96,384]{2,0,1:T(8,128)(2,1)}, u32[]{:S(2)}, u32[]{:S(2)}) %all-to-all-start.6) | async-done | bytes 3538976 | tf_op jit(solution)/shard_map/all_to_all | solution.py:271
  1423.2 13.1 reshape.7127
  1466.4 32.9 %fusion.251 = (u16[768,384]{1,0:T(8,128)(2,1)S(1)}, u16[768,384]{1,0:T(8,128)(2,1)S(1)}, u16[768,384]{1,0:T(8,128)(2,1)S(1)}, u16[768,384]{1,0:T(8,128)(2,1)S(1)...) fusion(f32[384]{0:T(512)S(1)} %convert_reduce_fusion.1, ...), kind=kOutput, calls=%fused_computation.617 | convolution fusion | flops 1561853952 | bytes 68643072 | tf_op jit(solution)/shard_map/acn,ch->anh/dot_general | solution.py:286
  1499.3 37.1 %fusion.246 = bf16[12,192,768]{2,1,0:T(8,128)(2,1)} fusion(f32[12,192,768]{2,1,0:T(8,128)} %copy-done.21, f32[12,768,384]{2,1,0:T(8,128)} %get-tuple-element.1155, f32[384]{0:T(512)S(1)} %convert_reduce_fusion.1, u16[768,384]{1,0:T(8,128)(2,1)S(1)} %get-tuple-element.775, u16[768,384]{1,0:T(8,128)(2,1)S(1)} %get-tuple-element.774, ...), kind=kOutput, calls=%fused_computation.603 | convolution fusion | flops 1613758464 | bytes 26101248 | tf_op jit(solution)/shard_map/anh,ch->acn/dot_general | solution.py:290
  1536.5 37.0 %fusion.243 = bf16[12,192,768]{2,1,0:T(8,128)(2,1)} fusion(f32[12,192,768]{2,1,0:T(8,128)} %copy-done.8, f32[12,768,384]{2,1,0:T(8,128)S(1)} %copy-done.18, f32[384]{0:T(512)S(1)} %convert_reduce_fusion.1, u16[768,384]{1,0:T(8,128)(2,1)S(1)} %get-tuple-element.782, u16[768,384]{1,0:T(8,128)(2,1)S(1)} %get-tuple-element.783, ...), kind=kOutput, calls=%fused_computation.597 | convolution fusion | flops 1613758464 | bytes 26101248 | tf_op jit(solution)/shard_map/anh,ch->acn/dot_general | solution.py:290
  1575.0 36.2 %fusion.244 = bf16[12,192,768]{2,1,0:T(8,128)(2,1)} fusion(f32[12,192,768]{2,1,0:T(8,128)S(1)} %copy-done.10, f32[12,768,384]{2,1,0:T(8,128)S(1)} %copy-done.17, f32[384]{0:T(512)S(1)} %convert_reduce_fusion.1, u16[768,384]{1,0:T(8,128)(2,1)} %get-tuple-element.784, u16[768,384]{1,0:T(8,128)(2,1)} %get-tuple-element.785, ...), kind=kOutput, calls=%fused_computation.599 | convolution fusion | flops 1613758464 | bytes 26101248 | tf_op jit(solution)/shard_map/anh,ch->acn/dot_general | solution.py:290
  1611.3 33.9 %fusion.245 = bf16[12,192,768]{2,1,0:T(8,128)(2,1)S(1)} fusion(f32[12,192,768]{2,1,0:T(8,128)S(1)} %copy-done.12, f32[12,768,384]{2,1,0:T(8,128)S(1)} %copy-done.16, f32[384]{0:T(512)S(1)} %convert_reduce_fusion.1, u16[768,384]{1,0:T(8,128)(2,1)S(1)} %copy-done.34, u16[768,384]{1,0:T(8,128)(2,1)S(1)} %copy-done.35, bf16[1,192,384]{2,1,0:T(8,128)(2,1)S(1)} %copy-done.32), kind=kOutput, calls=%fused_computation.601 | convolution fusion | flops 1613758464 | bytes 26101248 | tf_op jit(solution)/shard_map/anh,ch->acn/dot_general | solution.py:290
  1653.4 37.9 %collective-permute-done.2 = bf16[12,192,768]{2,1,0:T(8,128)(2,1)S(1)} collective-permute-done((bf16[12,192,768]{2,1,0:T(8,128)(2,1)S(1)}, bf16[12,192,768]{2,1,0:T(8,128)(2,1)S(1)}, u32[]{:S(2)}, u32[]{:S(2)}) %collective-permute-start.2) | collective-permute-done | bytes 3538976 | tf_op jit(solution)/shard_map/ppermute | solution.py:18
  (478 shorter events, 587.4 us)
Async XLA Ops:
  0.0 1446.2 %copy-start = (bf16[1,192,384]{2,1,0:T(8,128)(2,1)S(1)}, bf16[1,192,384]{2,1,0:T(8,128)(2,1)}, u32[]{:S(2)}) copy-start(bf16[1,192,384]{2,1,0:T(8,128)(2,1)} %param.18) | copy-start | bytes 442372
  0.0 70.3 %copy-start.25 = (s32[384]{0:T(512)}, s32[384]{0:T(512)S(1)}, u32[]{:S(2)}) copy-start(s32[384]{0:T(512)S(1)} %fusion.328) | copy-start | bytes 4612
  62.4 314.1 %all-to-all-start = ((bf16[384,48,384]{2,1,0:T(8,128)(2,1)}), bf16[384,48,384]{2,1,0:T(8,128)(2,1)}, u32[]{:S(2)}, u32[]{:S(2)}) async-start(bf16[384,48,384]{2,1,0:T(8,128)(2,1)} %copy.34), calls=%async_computation | async-start | bytes 28311552 | tf_op jit(solution)/shard_map/all_to_all | solution.py:210
  71.9 59.7 %copy-start.27 = (f32[384]{0:T(512)S(1)}, f32[384]{0:T(512)}, u32[]{:S(2)}) copy-start(f32[384]{0:T(512)} %sine_log_fusion) | copy-start | bytes 4612
  71.9 59.7 %copy-start.31 = (f32[48]{0:T(128)S(1)}, f32[48]{0:T(128)}, u32[]{:S(2)}) copy-start(f32[48]{0:T(128)} %add_multiply_fusion.16) | copy-start | bytes 580
  71.9 60.4 %copy-start.1 = (f32[24,48,384]{2,1,0:T(8,128)S(1)}, f32[24,48,384]{2,1,0:T(8,128)}, u32[]{:S(2)}) copy-start(f32[24,48,384]{2,1,0:T(8,128)} %custom-call.13) | copy-start | bytes 5308420
  71.9 60.4 %copy-start.19 = (f32[48,384]{1,0:T(8,128)S(1)}, f32[48,384]{1,0:T(8,128)}, u32[]{:S(2)}) copy-start(f32[48,384]{1,0:T(8,128)} %custom-call) | copy-start | bytes 221188
  72.0 60.4 %copy-start.20 = (f32[48,384]{1,0:T(8,128)S(1)}, f32[48,384]{1,0:T(8,128)}, u32[]{:S(2)}) copy-start(f32[48,384]{1,0:T(8,128)} %custom-call.1) | copy-start | bytes 221188
  190.4 100.2 %copy-start.24 = (pred[48,384]{1,0:T(8,128)(4,1)S(1)}, pred[48,384]{1,0:T(8,128)(4,1)}, u32[]{:S(2)}) copy-start(pred[48,384]{1,0:T(8,128)(4,1)} %iota_compare_fusion) | copy-start | bytes 55300
  438.5 246.6 %all-to-all-start.1 = ((bf16[408,24,384]{2,1,0:T(8,128)(2,1)}), bf16[408,24,384]{2,1,0:T(8,128)(2,1)}, u32[]{:S(2)}, u32[]{:S(2)}) async-start(bf16[408,24,384]{2,1,0:T(8,128)(2,1)} %slice_dynamic-update-slice_fusion.1), calls=%async_computation.1 | async-start | bytes 15040512 | tf_op jit(solution)/shard_map/all_to_all | solution.py:230
  447.5 197.0 %collective-permute-start = (bf16[24,192,384]{2,1,0:T(8,128)(2,1)}, bf16[24,192,384]{2,1,0:T(8,128)(2,1)}, u32[]{:S(2)}, u32[]{:S(2)}) collective-permute-start(bf16[24,192,384]{2,1,0:T(8,128)(2,1)} %slice_bitcast_fusion), channel_id=1, source_target_pairs={{0,7},{1,6},{2,5},{3,4},{4,3},{5,2},{6,1},{7,0},{8,15},{9,14},{10,... | collective-permute-start | bytes 10616840 | tf_op jit(solution)/shard_map/ppermute | solution.py:217
  1058.4 82.8 %all-to-all-start.5 = ((bf16[48,96,384]{2,0,1:T(8,128)(2,1)}), bf16[48,96,384]{2,0,1:T(8,128)(2,1)}, u32[]{:S(2)}, u32[]{:S(2)}) async-start(bf16[48,96,384]{2,0,1:T(8,128)(2,1)} %bitcast.605), calls=%async_computation.5 | async-start | bytes 7077888 | tf_op jit(solution)/shard_map/all_to_all | solution.py:271
  1141.2 83.0 %all-to-all-start.3 = ((bf16[48,96,384]{2,0,1:T(8,128)(2,1)}), bf16[48,96,384]{2,0,1:T(8,128)(2,1)}, u32[]{:S(2)}, u32[]{:S(2)}) async-start(bf16[48,96,384]{2,0,1:T(8,128)(2,1)} %bitcast.604), calls=%async_computation.3 | async-start | bytes 7077888 | tf_op jit(solution)/shard_map/all_to_all | solution.py:271
  1224.2 83.1 %all-to-all-start.6 = ((bf16[48,96,384]{2,0,1:T(8,128)(2,1)}), bf16[48,96,384]{2,0,1:T(8,128)(2,1)}, u32[]{:S(2)}, u32[]{:S(2)}) async-start(bf16[48,96,384]{2,0,1:T(8,128)(2,1)} %bitcast.603), calls=%async_computation.6 | async-start | bytes 7077888 | tf_op jit(solution)/shard_map/all_to_all | solution.py:271
  1307.4 106.3 %all-to-all-start.4 = ((bf16[48,96,384]{2,0,1:T(8,128)(2,1)}), bf16[48,96,384]{2,0,1:T(8,128)(2,1)}, u32[]{:S(2)}, u32[]{:S(2)}) async-start(bf16[48,96,384]{2,0,1:T(8,128)(2,1)} %bitcast.602), calls=%async_computation.4 | async-start | bytes 7077888 | tf_op jit(solution)/shard_map/all_to_all | solution.py:271
  1499.3 37.1 %copy-start.18 = (f32[12,768,384]{2,1,0:T(8,128)S(1)}, f32[12,768,384]{2,1,0:T(8,128)}, u32[]{:S(2)}) copy-start(f32[12,768,384]{2,1,0:T(8,128)} %fusion.266) | copy-start | bytes 42467332
  1536.4 109.5 %collective-permute-start.1 = (bf16[12,192,768]{2,1,0:T(8,128)(2,1)}, bf16[12,192,768]{2,1,0:T(8,128)(2,1)}, u32[]{:S(2)}, u32[]{:S(2)}) collective-permute-start(bf16[12,192,768]{2,1,0:T(8,128)(2,1)} %fusion.246), channel_id=1, source_target_pairs={{0,8},{8,16},{16,24},{24,0},{1,9},{9,17},{17,25},{25,1},{2,10},{10... | collective-permute-start | bytes 10616840 | tf_op jit(solution)/shard_map/ppermute | solution.py:18
  1536.4 38.6 %copy-start.10 = (f32[12,192,768]{2,1,0:T(8,128)S(1)}, f32[12,192,768]{2,1,0:T(8,128)}, u32[]{:S(2)}) copy-start(f32[12,192,768]{2,1,0:T(8,128)} %copy-done.9) | copy-start | bytes 21233668
  1536.4 38.6 %copy-start.17 = (f32[12,768,384]{2,1,0:T(8,128)S(1)}, f32[12,768,384]{2,1,0:T(8,128)}, u32[]{:S(2)}) copy-start(f32[12,768,384]{2,1,0:T(8,128)} %fusion.265) | copy-start | bytes 42467332
  1573.4 72.5 %collective-permute-start.4 = (bf16[12,192,768]{2,1,0:T(8,128)(2,1)}, bf16[12,192,768]{2,1,0:T(8,128)(2,1)}, u32[]{:S(2)}, u32[]{:S(2)}) collective-permute-start(bf16[12,192,768]{2,1,0:T(8,128)(2,1)} %fusion.243), channel_id=1, source_target_pairs={{0,8},{8,16},{16,24},{24,0},{1,9},{9,17},{17,25},{25,1},{2,10},{10... | collective-permute-start | bytes 10616840 | tf_op jit(solution)/shard_map/ppermute | solution.py:18
  1575.0 36.3 %copy-start.12 = (f32[12,192,768]{2,1,0:T(8,128)S(1)}, f32[12,192,768]{2,1,0:T(8,128)}, u32[]{:S(2)}) copy-start(f32[12,192,768]{2,1,0:T(8,128)} %copy-done.11) | copy-start | bytes 21233668
  1575.0 36.3 %copy-start.16 = (f32[12,768,384]{2,1,0:T(8,128)S(1)}, f32[12,768,384]{2,1,0:T(8,128)}, u32[]{:S(2)}) copy-start(f32[12,768,384]{2,1,0:T(8,128)} %fusion.264) | copy-start | bytes 42467332
  1611.3 42.1 %collective-permute-start.3 = (bf16[12,192,768]{2,1,0:T(8,128)(2,1)}, bf16[12,192,768]{2,1,0:T(8,128)(2,1)S(1)}, u32[]{:S(2)}, u32[]{:S(2)}) collective-permute-start(bf16[12,192,768]{2,1,0:T(8,128)(2,1)} %fusion.244), channel_id=1, source_target_pairs={{0,8},{8,16},{16,24},{24,0},{1,9},{9,17},{17,25},{25,1},{2,10},{10... | collective-permute-start | bytes 10616840 | tf_op jit(solution)/shard_map/ppermute | solution.py:18
  1645.2 46.1 %collective-permute-start.2 = (bf16[12,192,768]{2,1,0:T(8,128)(2,1)S(1)}, bf16[12,192,768]{2,1,0:T(8,128)(2,1)S(1)}, u32[]{:S(2)}, u32[]{:S(2)}) collective-permute-start(bf16[12,192,768]{2,1,0:T(8,128)(2,1)S(1)} %fusion.245), channel_id=1, source_target_pairs={{0,8},{8,16},{16,24},{24,0},{1,9},{9,17},{17,25},{25,1},{2,10},{10... | collective-permute-start | bytes 10616840 | tf_op jit(solution)/shard_map/ppermute | solution.py:18
  (33 other events, 245.8 us)
where the time goes:
time: 1710 us; the launch traced here: 1700 us
  waiting for transfers between devices  554 us (32%)
  matrix products  298 us (17%)
  other arithmetic  291 us (17%)
  local copies, waits for them, and re-layouts  264 us (15%)
  blocking collectives  253 us (15%)
  starting transfers between devices  37.7 us (2%)
    all_to_all x1, blocking collectives, shards(): lax.all_to_all(mixed.reshape(sp_count * slots, half, width), 'sp', split_...  253 us
    all_to_all x4, waiting for transfers between devices, shards(): lax.all_to_all(grid_part[:, :, start:start + chunk].reshape(modes_dev, sp...  216 us
    ppermute x1, waiting for transfers between devices, shards(): other_weight = lax.ppermute(own_weight[half:], 'sp', partner)  191 us
    dot_general x4, matrix products, shards(): jnp.einsum('anh,ch->acn', hidden, down_weight[0], preferred_element_type=...  144 us
    reshape x8, local copies, waits for them, and re-layouts, shards(): on_grid.reshape(MMAX, chunk, 2, C)  90.3 us
    unnamed x104, local copies, waits for them, and re-layouts  87.1 us
    all_to_all x1, waiting for transfers between devices, shards(): lax.all_to_all(spectral, 'sp', split_axis=0, concat_axis=1, tiled=True)  71.5 us
    while x14, other arithmetic  69.9 us
  transfers between devices with their start and end apart: 11, of which 8 were waited for; matrix products, arithmetic and copies ran while one was open for 27% of the time, Pallas kernels for 0%

commit v1 on v0

--- a/solution.py
+++ b/solution.py
@@ -207,7 +207,10 @@
     coeffs = jnp.einsum(
         "mla,mak->mlk",
         legendre,
-        lax.all_to_all(spectral, "sp", split_axis=0, concat_axis=1, tiled=True),
+        jnp.concatenate(
+            lax.all_to_all(jnp.stack(jnp.split(spectral, lax.axis_size("sp"), axis=0)), "sp", 0, 0),
+            axis=1,
+        ),
         preferred_element_type=jnp.float32,
     ).astype(jnp.bfloat16)
     half = LMAX // sp_count // 2

time: 1710 us -> 1790 us (1.047)
  local copies, waits for them, and re-layouts: 264 us -> 337 us
    another operation x0 -> x9, local copies, waits for them, and re-layouts: none -> 48.8 us  [shards(): jnp.stack(jnp.split(spectral, lax.axis_size('sp'), axis=0))]
    split x0 -> x1, local copies, waits for them, and re-layouts: none -> 31.7 us  [shards(): jnp.split(spectral, lax.axis_size('sp'), axis=0)]
    unnamed x104 -> x133, local copies, waits for them, and re-layouts: 87.1 us -> 98.3 us
  transfers between devices with their start and end apart: 11 -> 11, of which waited for: 8 -> 8; matrix products, arithmetic and copies ran while one was open for 27% -> 26% of each run, Pallas kernels for 0% -> 0%
where the time goes in v1:
time: 1790 us; the launch traced here: 1770 us
  waiting for transfers between devices  558 us (31%)
  local copies, waits for them, and re-layouts  337 us (19%)
  matrix products  296 us (17%)
  other arithmetic  289 us (16%)
  blocking collectives  252 us (14%)
  starting transfers between devices  37.4 us (2%)
    all_to_all x1, blocking collectives, shards(): lax.all_to_all(mixed.reshape(sp_count * slots, half, width), 'sp', split_...  252 us
    all_to_all x4, waiting for transfers between devices, shards(): lax.all_to_all(grid_part[:, :, start:start + chunk].reshape(modes_dev, sp...  216 us
    ppermute x1, waiting for transfers between devices, shards(): other_weight = lax.ppermute(own_weight[half:], 'sp', partner)  191 us
    dot_general x4, matrix products, shards(): jnp.einsum('anh,ch->acn', hidden, down_weight[0], preferred_element_type=...  142 us
    unnamed x133, local copies, waits for them, and re-layouts  98.3 us
    reshape x8, local copies, waits for them, and re-layouts, shards(): on_grid.reshape(MMAX, chunk, 2, C)  90.4 us
    all_to_all x1, waiting for transfers between devices, shards(): lax.all_to_all(jnp.stack(jnp.split(spectral, lax.axis_size('sp'), axis=0)...  71.7 us
    while x14, other arithmetic  69.6 us
  transfers between devices with their start and end apart: 11, of which 8 were waited for; matrix products, arithmetic and copies ran while one was open for 26% of the time, Pallas kernels for 0%

profile of v1, /device:TPU:0, one launch (start us, length us, event | category | flops | bytes accessed | tf_op | source)
XLA Modules:
  0.0 1773.2 jit_solution(6231631528856129694)
XLA Ops:
  24.5 19.0 %fusion.199 = bf16[384,48,2,192]{0,3,2,1:T(8,128)(2,1)} fusion(f32[48]{0:T(128)S(1)} %subtract_multiply_fusion, bf16[1,48,192,768]{3,2,1,0:T(8,128)(2,1)} %param.14, f32[192]{0:T(256)S(1)} %bitcast.634, f32[48,768]{1,0:T(8,128)S(1)} %add_rsqrt_fusion, f32[48,768]{1,0:T(8,128)S(1)} %broadcast_multiply_fusion, ...), kind=kOutput, calls=%fused_computation.502 | convolution fusion | flops 10923540480 | bytes 29787072 | tf_op jit(solution)/shard_map/nrm,acn->marc/dot_general | solution.py:201
  43.5 31.7 %fusion.484 = (bf16[48,48,2,192]{0,3,2,1:T(8,128)(2,1)}, bf16[48,48,2,192]{0,3,2,1:T(8,128)(2,1)}, bf16[48,48,2,192]{0,3,2,1:T(8,128)(2,1)}, bf16[48,48,2,192]{0...) fusion(bf16[384,48,2,192]{0,3,2,1:T(8,128)(2,1)} %fusion.199), kind=kLoop, calls=%fused_computation.926 | loop fusion | bytes 28311552 | tf_op jit(solution)/shard_map/split | solution.py:211
  145.0 59.4 %while.70 = (s32[]{:T(128)}, f32[24,48,384]{2,1,0:T(8,128)}, f32[24,48,384]{2,1,0:T(8,128)}, f32[24,48,384]{2,1,0:T(8,128)}, f32[24,48,384]{2,1,0:T(8,128)}, /*i...) while((s32[]{:T(128)}, f32[24,48,384]{2,1,0:T(8,128)}, ...), condition=%wide.region_2.3_spmd.clone.clone, body=%wide.region_1.2_spmd.clone.clone.sunk | while | flops 123129520 | bytes 200388496 | solution.py:107
  205.1 58.0 %while.69 = (s32[]{:T(128)}, f32[48,384]{1,0:T(8,128)S(1)}, f32[48,384]{1,0:T(8,128)S(1)}, f32[48,384]{1,0:T(8,128)S(1)}, f32[24,48,384]{2,1,0:T(8,128)}, /*inde...) while((s32[]{:T(128)}, f32[48,384]{1,0:T(8,128)S(1)}, ...), condition=%wide.region_4.5_spmd.clone, body=%wide.region_3.4_spmd.clone.sunk | while | flops 368643 | bytes 1548453 | solution.py:123
  263.1 100.4 %while.68 = (s32[]{:T(128)}, f32[24,48,384]{2,1,0:T(8,128)}, f32[24,48,384]{2,1,0:T(8,128)}, f32[24,48,384]{2,1,0:T(8,128)S(1)}, bf16[2,8,24,48,384]{4,1,0,2,3:T...) while((s32[]{:T(128)}, f32[24,48,384]{2,1,0:T(8,128)}, ...), condition=%wide.region_6.7_spmd.clone.clone, body=%wide.region_5.6_spmd.clone.clone.sunk | while | flops 100568752 | bytes 101660528 | solution.py:140
  363.5 14.3 fusion.186
  377.8 71.7 %all-to-all-done = bf16[8,48,48,384]{3,2,1,0:T(8,128)(2,1)} async-done(((bf16[8,48,48,384]{3,2,1,0:T(8,128)(2,1)}), bf16[8,48,48,384]{3,2,1,0:T(8,128)(2,1)}, u32[]{:S(2)}, u32[]{:S(2)}) %all-to-all-start) | async-done | bytes 14155808 | tf_op jit(solution)/shard_map/all_to_all | solution.py:211
  462.4 19.5 %convolution_convert_fusion.1 = bf16[48,384,384]{2,1,0:T(8,128)(2,1)} fusion(bf16[48,384,384]{2,1,0:T(8,128)(2,1)} %fusion.186, bf16[48,384,384]{2,1,0:T(8,128)(2,1)} %bitcast.584), kind=kOutput, calls=%fused_computation.579 | convolution fusion | flops 5442895872 | bytes 42467328 | tf_op jit(solution)/shard_map/mla,mak->mlk/dot_general | solution.py:207
  526.3 191.1 %collective-permute-done = bf16[24,192,384]{2,1,0:T(8,128)(2,1)} collective-permute-done((bf16[24,192,384]{2,1,0:T(8,128)(2,1)}, bf16[24,192,384]{2,1,0:T(8,128)(2,1)}, u32[]{:S(2)}, u32[]{:S(2)}) %collective-permute-start) | collective-permute-done | bytes 3538976 | tf_op jit(solution)/shard_map/ppermute | solution.py:220
  727.2 30.7 %all-to-all-done.1 = bf16[408,24,384]{2,1,0:T(8,128)(2,1)} async-done(((bf16[408,24,384]{2,1,0:T(8,128)(2,1)}), bf16[408,24,384]{2,1,0:T(8,128)(2,1)}, u32[]{:S(2)}, u32[]{:S(2)}) %all-to-all-start.1) | async-done | bytes 7520288 | tf_op jit(solution)/shard_map/all_to_all | solution.py:233
  769.9 14.5 fusion.238
  824.0 251.8 %all_to_all.75 = bf16[408,24,384]{2,1,0:T(8,128)(2,1)S(1)} all-to-all(bf16[408,24,384]{2,1,0:T(8,128)(2,1)S(1)} %bitcast.601), channel_id=1, replica_groups=mesh['section'=4,'sp'=8] {'sp'}, dimensions={0} | all-to-all | bytes 15040512 | tf_op jit(solution)/shard_map/all_to_all | solution.py:253
  1092.4 19.3 %convolution_convert_fusion = bf16[48,384,384]{2,1,0:T(8,128)(2,1)} fusion(bf16[48,384,384]{2,1,0:T(8,128)(2,1)} %fusion.186, bf16[48,384,384]{2,1,0:T(8,128)(2,1)} %fusion.308), kind=kOutput, calls=%fused_computation.578 | convolution fusion | flops 5442895872 | bytes 42467328 | tf_op jit(solution)/shard_map/mla,mlk->mak/dot_general | solution.py:267
  1111.7 14.2 fusion.483
  1140.4 72.1 %all-to-all-done.5 = bf16[48,96,384]{2,0,1:T(8,128)(2,1)} async-done(((bf16[48,96,384]{2,0,1:T(8,128)(2,1)}), bf16[48,96,384]{2,0,1:T(8,128)(2,1)}, u32[]{:S(2)}, u32[]{:S(2)}) %all-to-all-start.5) | async-done | bytes 3538976 | tf_op jit(solution)/shard_map/all_to_all | solution.py:274
  1223.4 72.1 %all-to-all-done.3 = bf16[48,96,384]{2,0,1:T(8,128)(2,1)} async-done(((bf16[48,96,384]{2,0,1:T(8,128)(2,1)}), bf16[48,96,384]{2,0,1:T(8,128)(2,1)}, u32[]{:S(2)}, u32[]{:S(2)}) %all-to-all-start.3) | async-done | bytes 3538976 | tf_op jit(solution)/shard_map/all_to_all | solution.py:274
  1306.3 72.2 %all-to-all-done.6 = bf16[48,96,384]{2,0,1:T(8,128)(2,1)} async-done(((bf16[48,96,384]{2,0,1:T(8,128)(2,1)}), bf16[48,96,384]{2,0,1:T(8,128)(2,1)}, u32[]{:S(2)}, u32[]{:S(2)}) %all-to-all-start.6) | async-done | bytes 3538976 | tf_op jit(solution)/shard_map/all_to_all | solution.py:274
  1443.2 13.3 reshape.7149
  1537.8 33.1 %fusion.252 = (u16[768,384]{1,0:T(8,128)(2,1)}, u16[768,384]{1,0:T(8,128)(2,1)}, u16[768,384]{1,0:T(8,128)(2,1)}, u16[768,384]{1,0:T(8,128)(2,1)}, u16[768,384]{...) fusion(f32[384]{0:T(512)S(1)} %convert_reduce_fusion.1, ...), kind=kOutput, calls=%fused_computation.618 | convolution fusion | flops 1561853952 | bytes 68643072 | tf_op jit(solution)/shard_map/acn,ch->anh/dot_general | solution.py:289
  1570.9 37.6 %fusion.247 = bf16[12,192,768]{2,1,0:T(8,128)(2,1)} fusion(f32[12,192,768]{2,1,0:T(8,128)} %copy-done.20, f32[12,768,384]{2,1,0:T(8,128)} %get-tuple-element.1163, f32[384]{0:T(512)S(1)} %convert_reduce_fusion.1, u16[768,384]{1,0:T(8,128)(2,1)} %get-tuple-element.775, u16[768,384]{1,0:T(8,128)(2,1)} %get-tuple-element.774, ...), kind=kOutput, calls=%fused_computation.604 | convolution fusion | flops 1613758464 | bytes 26101248 | tf_op jit(solution)/shard_map/anh,ch->acn/dot_general | solution.py:293
  1608.6 34.7 %fusion.244 = bf16[12,192,768]{2,1,0:T(8,128)(2,1)} fusion(f32[12,192,768]{2,1,0:T(8,128)S(1)} %bitcast.605, f32[12,768,384]{2,1,0:T(8,128)S(1)} %copy-done.17, f32[384]{0:T(512)S(1)} %convert_reduce_fusion.1, u16[768,384]{1,0:T(8,128)(2,1)S(1)} %copy-done.43, u16[768,384]{1,0:T(8,128)(2,1)S(1)} %copy-done.44, bf16[1,192,384]{2,1,0:T(8,128)(2,1)S(1)} %copy-done.37), kind=kOutput, calls=%fused_computation.598 | convolution fusion | flops 1613758464 | bytes 26101248 | tf_op jit(solution)/shard_map/anh,ch->acn/dot_general | solution.py:293
  1644.9 36.0 %fusion.245 = bf16[12,192,768]{2,1,0:T(8,128)(2,1)S(1)} fusion(f32[12,192,768]{2,1,0:T(8,128)S(1)} %copy-done.10, f32[12,768,384]{2,1,0:T(8,128)} %fusion.266, f32[384]{0:T(512)S(1)} %convert_reduce_fusion.1, u16[768,384]{1,0:T(8,128)(2,1)S(1)} %copy-done.41, u16[768,384]{1,0:T(8,128)(2,1)S(1)} %copy-done.42, bf16[1,192,384]{2,1,0:T(8,128)(2,1)S(1)} %copy-done.37), kind=kOutput, calls=%fused_computation.600 | convolution fusion | flops 1613758464 | bytes 26101248 | tf_op jit(solution)/shard_map/anh,ch->acn/dot_general | solution.py:293
  1681.0 33.9 %fusion.246 = bf16[12,192,768]{2,1,0:T(8,128)(2,1)S(1)} fusion(f32[12,192,768]{2,1,0:T(8,128)S(1)} %copy-done.12, f32[12,768,384]{2,1,0:T(8,128)S(1)} %copy-done.16, f32[384]{0:T(512)S(1)} %convert_reduce_fusion.1, u16[768,384]{1,0:T(8,128)(2,1)S(1)} %copy-done.39, u16[768,384]{1,0:T(8,128)(2,1)S(1)} %copy-done.40, bf16[1,192,384]{2,1,0:T(8,128)(2,1)S(1)} %copy-done.37), kind=kOutput, calls=%fused_computation.602 | convolution fusion | flops 1613758464 | bytes 26101248 | tf_op jit(solution)/shard_map/anh,ch->acn/dot_general | solution.py:293
  1725.5 37.9 %collective-permute-done.2 = bf16[12,192,768]{2,1,0:T(8,128)(2,1)S(1)} collective-permute-done((bf16[12,192,768]{2,1,0:T(8,128)(2,1)S(1)}, bf16[12,192,768]{2,1,0:T(8,128)(2,1)S(1)}, u32[]{:S(2)}, u32[]{:S(2)}) %collective-permute-start.2) | collective-permute-done | bytes 3538976 | tf_op jit(solution)/shard_map/ppermute | solution.py:18
  (517 shorter events, 648.2 us)
Async XLA Ops:
  0.0 1517.5 %copy-start = (bf16[1,192,384]{2,1,0:T(8,128)(2,1)S(1)}, bf16[1,192,384]{2,1,0:T(8,128)(2,1)}, u32[]{:S(2)}) copy-start(bf16[1,192,384]{2,1,0:T(8,128)(2,1)} %param.18) | copy-start | bytes 442372
  0.0 143.4 %copy-start.30 = (s32[384]{0:T(512)}, s32[384]{0:T(512)S(1)}, u32[]{:S(2)}) copy-start(s32[384]{0:T(512)S(1)} %fusion.329) | copy-start | bytes 4612
  135.4 314.1 %all-to-all-start = ((bf16[8,48,48,384]{3,2,1,0:T(8,128)(2,1)}), bf16[8,48,48,384]{3,2,1,0:T(8,128)(2,1)}, u32[]{:S(2)}, u32[]{:S(2)}) async-start(bf16[8,48,48,384]{3,2,1,0:T(8,128)(2,1)} %constant_dynamic-update-slice_fusion), calls=%async_computation | async-start | bytes 28311552 | tf_op jit(solution)/shard_map/all_to_all | solution.py:211
  144.9 59.4 %copy-start.32 = (f32[384]{0:T(512)S(1)}, f32[384]{0:T(512)}, u32[]{:S(2)}) copy-start(f32[384]{0:T(512)} %sine_log_fusion) | copy-start | bytes 4612
  144.9 59.4 %copy-start.36 = (f32[48]{0:T(128)S(1)}, f32[48]{0:T(128)}, u32[]{:S(2)}) copy-start(f32[48]{0:T(128)} %add_multiply_fusion.16) | copy-start | bytes 580
  144.9 60.1 %copy-start.1 = (f32[24,48,384]{2,1,0:T(8,128)S(1)}, f32[24,48,384]{2,1,0:T(8,128)}, u32[]{:S(2)}) copy-start(f32[24,48,384]{2,1,0:T(8,128)} %custom-call.14) | copy-start | bytes 5308420
  144.9 60.1 %copy-start.18 = (f32[48,384]{1,0:T(8,128)S(1)}, f32[48,384]{1,0:T(8,128)}, u32[]{:S(2)}) copy-start(f32[48,384]{1,0:T(8,128)} %custom-call) | copy-start | bytes 221188
  144.9 60.1 %copy-start.19 = (f32[48,384]{1,0:T(8,128)S(1)}, f32[48,384]{1,0:T(8,128)}, u32[]{:S(2)}) copy-start(f32[48,384]{1,0:T(8,128)} %custom-call.1) | copy-start | bytes 221188
  263.1 100.4 %copy-start.29 = (pred[48,384]{1,0:T(8,128)(4,1)S(1)}, pred[48,384]{1,0:T(8,128)(4,1)}, u32[]{:S(2)}) copy-start(pred[48,384]{1,0:T(8,128)(4,1)} %iota_compare_fusion) | copy-start | bytes 55300
  511.3 246.5 %all-to-all-start.1 = ((bf16[408,24,384]{2,1,0:T(8,128)(2,1)}), bf16[408,24,384]{2,1,0:T(8,128)(2,1)}, u32[]{:S(2)}, u32[]{:S(2)}) async-start(bf16[408,24,384]{2,1,0:T(8,128)(2,1)} %slice_dynamic-update-slice_fusion.1), calls=%async_computation.1 | async-start | bytes 15040512 | tf_op jit(solution)/shard_map/all_to_all | solution.py:233
  520.4 197.0 %collective-permute-start = (bf16[24,192,384]{2,1,0:T(8,128)(2,1)}, bf16[24,192,384]{2,1,0:T(8,128)(2,1)}, u32[]{:S(2)}, u32[]{:S(2)}) collective-permute-start(bf16[24,192,384]{2,1,0:T(8,128)(2,1)} %slice_bitcast_fusion), channel_id=1, source_target_pairs={{0,7},{1,6},{2,5},{3,4},{4,3},{5,2},{6,1},{7,0},{8,15},{9,14},{10,... | collective-permute-start | bytes 10616840 | tf_op jit(solution)/shard_map/ppermute | solution.py:220
  1129.7 82.8 %all-to-all-start.5 = ((bf16[48,96,384]{2,0,1:T(8,128)(2,1)}), bf16[48,96,384]{2,0,1:T(8,128)(2,1)}, u32[]{:S(2)}, u32[]{:S(2)}) async-start(bf16[48,96,384]{2,0,1:T(8,128)(2,1)} %bitcast.619), calls=%async_computation.5 | async-start | bytes 7077888 | tf_op jit(solution)/shard_map/all_to_all | solution.py:274
  1212.5 83.1 %all-to-all-start.3 = ((bf16[48,96,384]{2,0,1:T(8,128)(2,1)}), bf16[48,96,384]{2,0,1:T(8,128)(2,1)}, u32[]{:S(2)}, u32[]{:S(2)}) async-start(bf16[48,96,384]{2,0,1:T(8,128)(2,1)} %bitcast.618), calls=%async_computation.3 | async-start | bytes 7077888 | tf_op jit(solution)/shard_map/all_to_all | solution.py:274
  1295.5 83.0 %all-to-all-start.6 = ((bf16[48,96,384]{2,0,1:T(8,128)(2,1)}), bf16[48,96,384]{2,0,1:T(8,128)(2,1)}, u32[]{:S(2)}, u32[]{:S(2)}) async-start(bf16[48,96,384]{2,0,1:T(8,128)(2,1)} %bitcast.617), calls=%async_computation.6 | async-start | bytes 7077888 | tf_op jit(solution)/shard_map/all_to_all | solution.py:274
  1378.5 106.5 %all-to-all-start.4 = ((bf16[48,96,384]{2,0,1:T(8,128)(2,1)}), bf16[48,96,384]{2,0,1:T(8,128)(2,1)}, u32[]{:S(2)}, u32[]{:S(2)}) async-start(bf16[48,96,384]{2,0,1:T(8,128)(2,1)} %bitcast.616), calls=%async_computation.4 | async-start | bytes 7077888 | tf_op jit(solution)/shard_map/all_to_all | solution.py:274
  1537.8 70.7 %slice-start.2 = ((s8[7077888]{0:T(1024)(128)(4,1)}), s8[2883584]{0:T(1024)(128)(4,1)S(1)}, s32[]{:S(2)}) async-start(s8[7077888]{0:T(1024)(128)(4,1)} %bitcast.604), calls=%async_computation.9 | async-start | bytes 5767168
  1570.9 37.6 %slice-start.3 = ((s8[7077888]{0:T(1024)(128)(4,1)}), s8[4194304]{0:T(1024)(128)(4,1)S(1)}, s32[]{:S(2)}) async-start(s8[7077888]{0:T(1024)(128)(4,1)} %bitcast.604), calls=%async_computation.10 | async-start | bytes 8388608
  1570.9 37.6 %copy-start.17 = (f32[12,768,384]{2,1,0:T(8,128)S(1)}, f32[12,768,384]{2,1,0:T(8,128)}, u32[]{:S(2)}) copy-start(f32[12,768,384]{2,1,0:T(8,128)} %fusion.267) | copy-start | bytes 42467332
  1570.9 37.6 %copy-start.43 = (u16[768,384]{1,0:T(8,128)(2,1)S(1)}, u16[768,384]{1,0:T(8,128)(2,1)}, u32[]{:S(2)}) copy-start(u16[768,384]{1,0:T(8,128)(2,1)} %get-tuple-element.782) | copy-start | bytes 1769476
  1570.9 37.6 %copy-start.44 = (u16[768,384]{1,0:T(8,128)(2,1)S(1)}, u16[768,384]{1,0:T(8,128)(2,1)}, u32[]{:S(2)}) copy-start(u16[768,384]{1,0:T(8,128)(2,1)} %get-tuple-element.783) | copy-start | bytes 1769476
  1608.5 107.1 %collective-permute-start.1 = (bf16[12,192,768]{2,1,0:T(8,128)(2,1)}, bf16[12,192,768]{2,1,0:T(8,128)(2,1)}, u32[]{:S(2)}, u32[]{:S(2)}) collective-permute-start(bf16[12,192,768]{2,1,0:T(8,128)(2,1)} %fusion.247), channel_id=1, source_target_pairs={{0,8},{8,16},{16,24},{24,0},{1,9},{9,17},{17,25},{25,1},{2,10},{10... | collective-permute-start | bytes 10616840 | tf_op jit(solution)/shard_map/ppermute | solution.py:18
  1643.3 72.3 %collective-permute-start.4 = (bf16[12,192,768]{2,1,0:T(8,128)(2,1)}, bf16[12,192,768]{2,1,0:T(8,128)(2,1)}, u32[]{:S(2)}, u32[]{:S(2)}) collective-permute-start(bf16[12,192,768]{2,1,0:T(8,128)(2,1)} %fusion.244), channel_id=1, source_target_pairs={{0,8},{8,16},{16,24},{24,0},{1,9},{9,17},{17,25},{25,1},{2,10},{10... | collective-permute-start | bytes 10616840 | tf_op jit(solution)/shard_map/ppermute | solution.py:18
  1680.9 44.5 %collective-permute-start.3 = (bf16[12,192,768]{2,1,0:T(8,128)(2,1)S(1)}, bf16[12,192,768]{2,1,0:T(8,128)(2,1)S(1)}, u32[]{:S(2)}, u32[]{:S(2)}) collective-permute-start(bf16[12,192,768]{2,1,0:T(8,128)(2,1)S(1)} %fusion.245), channel_id=1, source_target_pairs={{0,8},{8,16},{16,24},{24,0},{1,9},{9,17},{17,25},{25,1},{2,10},{10... | collective-permute-start | bytes 10616840 | tf_op jit(solution)/shard_map/ppermute | solution.py:18
  1714.9 48.4 %collective-permute-start.2 = (bf16[12,192,768]{2,1,0:T(8,128)(2,1)S(1)}, bf16[12,192,768]{2,1,0:T(8,128)(2,1)S(1)}, u32[]{:S(2)}, u32[]{:S(2)}) collective-permute-start(bf16[12,192,768]{2,1,0:T(8,128)(2,1)S(1)} %fusion.246), channel_id=1, source_target_pairs={{0,8},{8,16},{16,24},{24,0},{1,9},{9,17},{17,25},{25,1},{2,10},{10... | collective-permute-start | bytes 10616840 | tf_op jit(solution)/shard_map/ppermute | solution.py:18
  (44 other events, 445.1 us)
